TPU v7x, 256 devices: a whole 4x4x8 slice. The times are simulated.
256 devices in a mesh: row: 16 (over z_lo, x, core), col: 16 (over y, z_hi).
Axes of the slice: x: 4, y: 4, z: 8 (z_hi: 4, z_lo: 2; z = z_hi * 2 + z_lo), core: 2. Of those that a mesh axis runs over, the one named last changes fastest.
Arguments:
- matrix_tiles: float32 [1, 16, 1, 16, 1024, 1024], P(None, 'row', None, 'col'), may hold values from -17 to 17, as said below
- panels: float32 [3, 1, 16, 512, 128], P(None, None, 'row', 'col'), may hold values from -0.25 to 0.25
- plan: int32 [3, 16], replicated, may hold values 0 or 1
Outputs:
- updated_tiles: float32 [1, 16, 1, 16, 1024, 1024], P(None, 'row', None, 'col')
Inputs may be any that keep to these rules, and one draw needn't show every extreme that they name: `matrix_tiles`: entries below the first subdiagonal of the matrix are zero.
All inputs are finite; a program needn't handle non-finite values.
Results may differ from a plain program's by a relative error of at most 0.0003.
Values sent between devices are 32-bit elements; how exact they have to be, the bound alone decides.
A program may use at most 64 MiB of HBM per device.

v0:
```python
import jax
import jax.numpy as jnp
from jax import lax
from jax.sharding import PartitionSpec as P

exact_mode = lax.Precision.HIGHEST


def broadcast(value, axis, source):
    kept = jnp.where(lax.axis_index(axis) == source, value, 0).astype(value.dtype)
    return lax.psum(kept, axis)


def passed_along(value, axis, steps):
    count = lax.axis_size(axis)
    pairs = [(source, (source + steps) % count) for source in range(count)]
    return lax.ppermute(value, axis, pairs)


def round_offsets(tile_size, window):
    return [0, tile_size - window // 2, window // 2]


def upper_inverse(upper_part):
    order_n = upper_part.shape[0]
    identity = jnp.eye(order_n, dtype=upper_part.dtype)
    scale = 1.0 / jnp.diag(upper_part)
    power = identity - upper_part * scale[:, None]
    result = identity + power
    span = 2
    while span < order_n:
        power = jnp.dot(power, power, precision=exact_mode)
        result = jnp.dot(result, identity + power, precision=exact_mode)
        span = span * 2
    return result * scale[None, :]


def window_factor(reflect):
    window, reflectors = reflect.shape
    gram_matrix = jnp.dot(reflect.T, reflect, precision=exact_mode)
    upper_part = jnp.triu(gram_matrix, 1) + jnp.diag(jnp.diag(gram_matrix) * 0.5)
    factor = upper_inverse(upper_part)
    product = jnp.dot(reflect, factor, precision=exact_mode)
    return jnp.eye(window, dtype=reflect.dtype) - jnp.dot(product, reflect.T, precision=exact_mode)


def live_mask(plan, tile_ids, offsets, window, tile_size):
    chosen = jnp.take(plan, tile_ids, axis=1) > 0
    inside = jnp.stack(
        [
            tile_ids < plan.shape[1] - 1 if offset + window > tile_size else tile_ids >= 0
            for offset in offsets
        ]
    )
    return jnp.logical_and(chosen, inside)


def on_device(matrix_tiles, panels, plan):
    rows_n = lax.axis_size("row")
    cols_n = lax.axis_size("col")
    row_at = lax.axis_index("row")
    col_at = lax.axis_index("col")
    row_tiles, _, col_tiles, _, tile_size, _ = matrix_tiles.shape
    rounds, _, _, _, reflectors = panels.shape
    matrix = matrix_tiles.reshape(row_tiles, col_tiles, tile_size, tile_size)
    gathered = lax.all_gather(panels, "col", axis=3, tiled=True)
    window = gathered.shape[3]
    half_width = window // 2
    panel_all = gathered.reshape(rounds, row_tiles, window, reflectors)
    offsets = round_offsets(tile_size, window)
    identity = jnp.eye(window, dtype=jnp.float32)
    factors = jax.vmap(window_factor)(panel_all.reshape(-1, window, reflectors)).reshape(
        rounds, row_tiles, window, window
    )
    left_ids = jnp.arange(row_tiles, dtype=jnp.int32) * rows_n + row_at
    left_live = live_mask(plan, left_ids, offsets, window, tile_size)
    left_q = jnp.where(left_live[:, :, None, None], factors, identity)
    right_ids = jnp.arange(col_tiles, dtype=jnp.int32) * cols_n + col_at
    source_row = col_at % rows_n
    picked = right_ids // rows_n
    received = broadcast(factors, "row", source_row)
    right_raw = jnp.take(received, picked, axis=1)
    right_live = live_mask(plan, right_ids, offsets, window, tile_size)
    right_q = jnp.where(right_live[:, :, None, None], right_raw, identity)
    last_row = row_at == rows_n - 1
    last_col = col_at == cols_n - 1
    for round_at in range(rounds):
        offset = offsets[round_at]
        left_now = left_q[round_at]
        right_now = right_q[round_at]
        if offset + window <= tile_size:
            window_rows = matrix[:, :, offset : offset + window, :]
            updated = jnp.einsum("ivw,ijvx->ijwx", left_now, window_rows, precision=exact_mode)
            matrix = matrix.at[:, :, offset : offset + window, :].set(updated)
            window_cols = matrix[:, :, :, offset : offset + window]
            updated = jnp.einsum("ijyv,jvw->ijyw", window_cols, right_now, precision=exact_mode)
            matrix = matrix.at[:, :, :, offset : offset + window].set(updated)
        else:
            from_below = passed_along(matrix[:, :, :half_width, :], "row", -1)
            from_below = jnp.where(last_row, jnp.roll(from_below, -1, axis=0), from_below)
            stacked = jnp.concatenate(
                [matrix[:, :, tile_size - half_width :, :], from_below], axis=2
            )
            updated = jnp.einsum("ivw,ijvx->ijwx", left_now, stacked, precision=exact_mode)
            going_back = updated[:, :, half_width:, :]
            going_back = jnp.where(last_row, jnp.roll(going_back, 1, axis=0), going_back)
            returned = passed_along(going_back, "row", 1)
            matrix = matrix.at[:, :, tile_size - half_width :, :].set(updated[:, :, :half_width, :])
            matrix = matrix.at[:, :, :half_width, :].set(returned)
            from_right = passed_along(matrix[:, :, :, :half_width], "col", -1)
            from_right = jnp.where(last_col, jnp.roll(from_right, -1, axis=1), from_right)
            stacked = jnp.concatenate(
                [matrix[:, :, :, tile_size - half_width :], from_right], axis=3
            )
            updated = jnp.einsum("ijyv,jvw->ijyw", stacked, right_now, precision=exact_mode)
            going_back = updated[:, :, :, half_width:]
            going_back = jnp.where(last_col, jnp.roll(going_back, 1, axis=1), going_back)
            returned = passed_along(going_back, "col", 1)
            matrix = matrix.at[:, :, :, tile_size - half_width :].set(updated[:, :, :, :half_width])
            matrix = matrix.at[:, :, :, :half_width].set(returned)
    return matrix.reshape(row_tiles, 1, col_tiles, 1, tile_size, tile_size)


def solution(mesh):
    placed = (P(None, "row", None, "col", None, None), P(None, None, "row", "col", None), P())
    return jax.shard_map(
        on_device,
        mesh=mesh,
        in_specs=placed,
        out_specs=P(None, "row", None, "col", None, None),
        check_vma=False,
    )
```

profile of v0, /device:TPU:39, one launch (start us, length us, event | category | flops | bytes accessed | tf_op | source)
XLA Modules:
  0.0 421.5 jit_solution(6370427126374975800)
XLA Ops:
  6.5 4.8 %copy.29 = f32[1,1,1,1,1024,1024]{5,4,3,2,1,0:T(8,128)} copy(f32[1,1,1,1,1024,1024]{5,4,3,2,1,0:T(8,128)} %param.21) | data formatting | bytes 8388608
  11.4 1.2 fusion.15
  12.6 45.0 %all_gather.3 = f32[3,1,1,512,128]{4,3,0,2,1:T(8,128)S(1)} all-gather(f32[3,1,1,32,128]{4,3,0,2,1:T(8,128)S(1)} %bitcast.123), channel_id=1, replica_groups=mesh['row'=16,'col'=16] {'col'}, dimensions={3}, use_global_device_ids=true | all-gather | bytes 835584 | tf_op jit(solution)/shard_map/all_gather | solution.py:66
  57.6 1.4 fusion.20
  59.0 4.6 %copy.6 = f32[3,128,128]{0,2,1:T(8,128)} copy(f32[3,128,128]{2,1,0:T(8,128)S(1)} %fusion.20) | data formatting | bytes 393216 | tf_op jit(solution)/shard_map/vmap()/dot_general | solution.py:40
  63.6 1.8 gather_fusion
  65.4 0.1 copy.7
  65.5 0.1 select_add_fusion
  65.6 5.1 %copy.8 = f32[3,128,128]{0,2,1:T(8,128)} copy(f32[3,128,128]{2,1,0:T(8,128)S(1)} %select_add_fusion) | data formatting | bytes 393216 | tf_op jit(solution)/shard_map/vmap()/add | solution.py:41
  70.7 1.8 gather_fusion.1
  72.5 0.1 copy.9
  72.6 0.4 fusion.33
  73.0 0.4 fusion.30
  73.4 0.3 fusion.59
  73.8 0.3 fusion.60
  74.1 0.3 fusion.28
  74.4 0.0 copy-start.4
  74.4 0.3 fusion.61
  74.8 0.3 fusion.26
  75.1 0.3 fusion.62
  75.4 0.3 fusion.24
  75.8 0.3 convolution_add_fusion
  76.1 0.3 fusion.22
  76.4 0.4 convolution_multiply_fusion
  76.8 0.8 fusion.18
  77.6 0.2 fusion.50
  77.8 5.7 %select_bitcast_fusion = (f32[3,1,512,512]{3,2,0,1:T(8,128)}, f32[3,512,512]{2,1,0:T(8,128)S(1)}) fusion(f32[512,512]{1,0:T(8,128)S(1)} %copy-done.2, pred[]{:T(512)S(6)} %eq.46, pred[3]{0:T(512)(128)(4,1)S(1)} %get-tuple-element.114, f32[3,128,512]{1,2,0:T(8,128)S(1)} %fusion.18, f32[3,1,1,512,128]{4,3,0,2,1:T(8,128)} %copy-done.1), kind=kOutput, calls=%fused_computation.3 | convolution fusion | flops 1210318848 | bytes 8912900 | tf_op jit(solution)/shard_map/vmap()/dot_general | solution.py:44
  83.5 0.0 all-reduce.2.cloned.1.call-update
  83.5 5.1 %fusion.3 = f32[512,1024]{1,0:T(8,128)S(1)} fusion(f32[1,1,1024,1024]{3,2,1,0:T(8,128)} %bitcast, f32[3,512,512]{2,1,0:T(8,128)S(1)} %get-tuple-element.120), kind=kOutput, calls=%fused_computation.12 | convolution fusion | flops 3221225472 | bytes 5242880 | tf_op jit(solution)/shard_map/ivw,ijvx->ijwx/dot_general | solution.py:93
  88.6 1.5 bitcast_dynamic-update-slice_fusion
  90.1 126.7 %all-reduce.2.cloned.1.call-done = f32[3,1,512,512]{3,2,0,1:T(8,128)} async-done(((f32[3,1,512,512]{3,2,0,1:T(8,128)}), f32[3,1,512,512]{3,2,0,1:T(8,128)}) %all-reduce.2.cloned.1.call-update) | async-done | bytes 3145744 | tf_op jit(solution)/shard_map/psum | solution.py:11
  216.8 2.8 select_select_fusion
  219.6 1.6 copy-done
  221.3 10.0 %fusion.12 = f32[1,1,1024,512]{2,3,0,1:T(8,128)} fusion(f32[1,1,1024,1024]{3,2,1,0:T(8,128)} %bitcast_dynamic-update-slice_fusion, f32[3,1,512,512]{3,2,0,1:T(8,128)S(1)} %select_select_fusion), kind=kOutput, calls=%fused_computation.24 | convolution fusion | flops 3221225472 | bytes 5242880 | tf_op jit(solution)/shard_map/ijyv,jvw->ijyw/dot_general | solution.py:96
  231.3 2.9 copy.11
  234.2 3.1 constant_dynamic-update-slice_fusion.6
  237.3 1.7 fusion.54
  238.9 0.1 collective-permute-start
  239.0 16.3 %collective-permute-done = f32[1,1,256,1024]{3,2,1,0:T(8,128)S(1)} collective-permute-done((f32[1,1,256,1024]{3,2,1,0:T(8,128)S(1)}, f32[1,1,256,1024]{3,2,1,0:T(8,128)S(1)}, u32[]{:S(2)}, u32[]{:S(2)}) %collective-permute-start) | collective-permute-done | bytes 1048608 | tf_op jit(solution)/shard_map/ppermute | solution.py:17
  255.3 3.5 fusion.11
  258.9 1.5 fusion.56
  260.3 0.2 collective-permute-start.1
  260.5 2.6 copy.12
  263.1 2.3 constant_dynamic-update-slice_fusion.5
  265.4 7.2 %collective-permute-done.1 = f32[1,1,256,1024]{2,3,1,0:T(8,128)} collective-permute-done((f32[1,1,256,1024]{2,3,1,0:T(8,128)}, f32[1,1,256,1024]{2,3,1,0:T(8,128)}, u32[]{:S(2)}, u32[]{:S(2)}) %collective-permute-start.1) | collective-permute-done | bytes 1048608 | tf_op jit(solution)/shard_map/ppermute | solution.py:17
  272.6 2.5 copy.13
  275.1 2.3 constant_dynamic-update-slice_fusion.4
  277.4 1.7 fusion.53
  279.1 5.2 %collective-permute-start.2 = (f32[1,1,1024,256]{3,2,1,0:T(8,128)S(1)}, f32[1,1,1024,256]{3,2,1,0:T(8,128)S(1)}, u32[]{:S(2)}, u32[]{:S(2)}) collective-permute-start(f32[1,1,1024,256]{3,2,1,0:T(8,128)S(1)} %get-tuple-element.116), channel_id=1, source_target_pairs={{0,15},{1,0},{2,1},{3,2},{4,3},{5,4},{6,5},{7,6},{8,7},{9,8},{10,9... | collective-permute-start | bytes 3145736 | tf_op jit(solution)/shard_map/ppermute | solution.py:17
  284.3 41.2 %collective-permute-done.2 = f32[1,1,1024,256]{3,2,1,0:T(8,128)S(1)} collective-permute-done((f32[1,1,1024,256]{3,2,1,0:T(8,128)S(1)}, f32[1,1,1024,256]{3,2,1,0:T(8,128)S(1)}, u32[]{:S(2)}, u32[]{:S(2)}) %collective-permute-start.2) | collective-permute-done | bytes 1048608 | tf_op jit(solution)/shard_map/ppermute | solution.py:17
  325.5 8.0 %fusion.10 = f32[1,1,1024,512]{2,3,0,1:T(8,128)S(1)} fusion(f32[1,1,1024,256]{3,2,1,0:T(8,128)S(1)} %collective-permute-done.2, f32[1,1,1024,256]{3,2,1,0:T(8,128)S(1)} %get-tuple-element.115, f32[3,1,512,512]{3,2,0,1:T(8,128)} %copy-done), kind=kOutput, calls=%fused_computation.22 | convolution fusion | flops 3221749760 | bytes 5242880 | tf_op jit(solution)/shard_map/ijyv,jvw->ijyw/dot_general | solution.py:115
  333.4 1.5 fusion.55
  334.9 0.2 collective-permute-start.3
  335.2 2.6 copy.14
  337.7 2.3 constant_dynamic-update-slice_fusion.3
  340.0 46.3 %collective-permute-done.3 = f32[1,1,1024,256]{2,3,0,1:T(8,128)} collective-permute-done((f32[1,1,1024,256]{2,3,0,1:T(8,128)}, f32[1,1,1024,256]{2,3,0,1:T(8,128)}, u32[]{:S(2)}, u32[]{:S(2)}) %collective-permute-start.3) | collective-permute-done | bytes 1048608 | tf_op jit(solution)/shard_map/ppermute | solution.py:17
  386.3 2.5 copy.15
  388.8 2.3 constant_dynamic-update-slice_fusion.2
  391.1 6.4 %fusion.13 = f32[1,1,512,1024]{2,3,1,0:T(8,128)} fusion(f32[1,1,1024,1024]{3,2,1,0:T(8,128)} %constant_dynamic-update-slice_fusion.2, f32[3,512,512]{2,1,0:T(8,128)S(1)} %get-tuple-element.120), kind=kOutput, calls=%fused_computation.25 | convolution fusion | flops 3221225472 | bytes 5242880 | tf_op jit(solution)/shard_map/ivw,ijvx->ijwx/dot_general | solution.py:93
  397.5 1.9 copy.16
  399.4 1.5 constant_dynamic-update-slice_fusion.1
  400.8 10.0 %fusion.14 = f32[1,1,1,1,1024,512]{4,5,3,2,1,0:T(8,128)} fusion(f32[1,1,1024,1024]{3,2,1,0:T(8,128)} %constant_dynamic-update-slice_fusion.1, f32[3,1,512,512]{3,2,0,1:T(8,128)} %copy-done), kind=kOutput, calls=%fused_computation.26 | convolution fusion | flops 3221225472 | bytes 5242880 | tf_op jit(solution)/shard_map/ijyv,jvw->ijyw/dot_general | solution.py:96
  410.8 1.9 copy.17
  412.7 1.5 constant_dynamic-update-slice_fusion
  (14 shorter events, 0.1 us)
Async XLA Ops:
  6.5 6.0 %copy-start.3 = (f32[3,1,1,32,128]{4,3,2,1,0:T(8,128)S(1)}, f32[3,1,1,32,128]{4,3,2,1,0:T(8,128)}, u32[]{:S(2)}) copy-start(f32[3,1,1,32,128]{4,3,2,1,0:T(8,128)} %param.22) | copy-start | bytes 147460
  6.5 210.3 %all-reduce.2.cloned.1.call-start = ((), (), s32[]{:S(2)}) async-start(), calls=%async_computation | async-start | bytes 6291456 | tf_op jit(solution)/shard_map/psum | solution.py:11
  57.6 19.2 %copy-start.1 = (f32[3,1,1,512,128]{4,3,0,2,1:T(8,128)}, f32[3,1,1,512,128]{4,3,0,2,1:T(8,128)S(1)}, u32[]{:S(2)}) copy-start(f32[3,1,1,512,128]{4,3,0,2,1:T(8,128)S(1)} %all_gather.3) | copy-start | bytes 2359300
  74.4 3.2 copy-start.4
  74.4 3.4 copy-start.2
  219.6 1.6 copy-start
  238.9 16.4 %collective-permute-start = (f32[1,1,256,1024]{3,2,1,0:T(8,128)S(1)}, f32[1,1,256,1024]{3,2,1,0:T(8,128)S(1)}, u32[]{:S(2)}, u32[]{:S(2)}) collective-permute-start(f32[1,1,256,1024]{3,2,1,0:T(8,128)S(1)} %get-tuple-element.118), channel_id=1, source_target_pairs={{0,240},{16,0},{32,16},{48,32},{64,48},{80,64},{96,80},{112,96},{1... | collective-permute-start | bytes 3145736 | tf_op jit(solution)/shard_map/ppermute | solution.py:17
  260.3 12.3 %collective-permute-start.1 = (f32[1,1,256,1024]{2,3,1,0:T(8,128)}, f32[1,1,256,1024]{2,3,1,0:T(8,128)}, u32[]{:S(2)}, u32[]{:S(2)}) collective-permute-start(f32[1,1,256,1024]{2,3,1,0:T(8,128)} %get-tuple-element.123), channel_id=1, source_target_pairs={{0,16},{16,32},{32,48},{48,64},{64,80},{80,96},{96,112},{112,128},... | collective-permute-start | bytes 3145736 | tf_op jit(solution)/shard_map/ppermute | solution.py:17
  279.1 46.4 %collective-permute-start.2 = (f32[1,1,1024,256]{3,2,1,0:T(8,128)S(1)}, f32[1,1,1024,256]{3,2,1,0:T(8,128)S(1)}, u32[]{:S(2)}, u32[]{:S(2)}) collective-permute-start(f32[1,1,1024,256]{3,2,1,0:T(8,128)S(1)} %get-tuple-element.116), channel_id=1, source_target_pairs={{0,15},{1,0},{2,1},{3,2},{4,3},{5,4},{6,5},{7,6},{8,7},{9,8},{10,9... | collective-permute-start | bytes 3145736 | tf_op jit(solution)/shard_map/ppermute | solution.py:17
  334.9 51.4 %collective-permute-start.3 = (f32[1,1,1024,256]{2,3,0,1:T(8,128)}, f32[1,1,1024,256]{2,3,0,1:T(8,128)}, u32[]{:S(2)}, u32[]{:S(2)}) collective-permute-start(f32[1,1,1024,256]{2,3,0,1:T(8,128)} %get-tuple-element.121), channel_id=1, source_target_pairs={{0,1},{1,2},{2,3},{3,4},{4,5},{5,6},{6,7},{7,8},{8,9},{9,10},{10,1... | collective-permute-start | bytes 3145736 | tf_op jit(solution)/shard_map/ppermute | solution.py:17
Sparse Core Ops, SparseCore 0:
  83.6 133.1 all-reduce.1
where the time goes:
time: 425 us; the launch traced here: 422 us
  waiting for transfers between devices  238 us (56%)
  local copies, waits for them, and re-layouts  59.7 us (14%)
  matrix products  54.8 us (13%)
  blocking collectives  45 us (11%)
  between operations  14.2 us (3%)
  starting transfers between devices  5.72 us (1%)
  other arithmetic  4.4 us (1%)
    psum x1, waiting for transfers between devices, broadcast(): return lax.psum(kept, axis)  127 us
    ppermute x4, waiting for transfers between devices, passed_along(): return lax.ppermute(value, axis, pairs)  111 us
    all_gather x1, blocking collectives, on_device(): gathered = lax.all_gather(panels, 'col', axis=3, tiled=True)  45 us
    dot_general x2, matrix products, on_device(): jnp.einsum('ijyv,jvw->ijyw', window_cols, right_now, precision=exact_mode)  20 us
    dot_general x2, matrix products, on_device(): jnp.einsum('ivw,ijvx->ijwx', left_now, window_rows, precision=exact_mode)  11.5 us
  transfers between devices with their start and end apart: 5, of which 5 were waited for; matrix products, arithmetic and copies ran while one was open for 4% of the time, Pallas kernels for 0%

commit v1 on v0

--- a/solution.py
+++ b/solution.py
@@ -63,7 +63,10 @@
     row_tiles, _, col_tiles, _, tile_size, _ = matrix_tiles.shape
     rounds, _, _, _, reflectors = panels.shape
     matrix = matrix_tiles.reshape(row_tiles, col_tiles, tile_size, tile_size)
-    gathered = lax.all_gather(panels, "col", axis=3, tiled=True)
+    size = lax.axis_size("col")
+    blocks = jnp.stack([panels for _ in range(size)])
+    blocks = lax.all_to_all(blocks, "col", split_axis=0, concat_axis=0)
+    gathered = jnp.concatenate(blocks, axis=3)
     window = gathered.shape[3]
     half_width = window // 2
     panel_all = gathered.reshape(rounds, row_tiles, window, reflectors)

time: 425 us -> 411 us (0.967); the launches traced: 422 us -> 403 us
  blocking collectives: 45 us -> 0 us
  waiting for transfers between devices: 238 us -> 253 us
  starting transfers between devices: 5.72 us -> 16 us
    all_gather x1 -> x0, blocking collectives: 45 us -> none  [on_device(): gathered = lax.all_gather(panels, 'col', axis=3, tiled=True)]
    all_to_all x0 -> x1, waiting for transfers between devices: none -> 21.2 us  [on_device(): blocks = lax.all_to_all(blocks, 'col', split_axis=0, concat_axis=0)]
    all_to_all x0 -> x1, starting transfers between devices: none -> 10 us  [on_device(): blocks = lax.all_to_all(blocks, 'col', split_axis=0, concat_axis=0)]
    psum x1, waiting for transfers between devices: 127 us -> 121 us  [broadcast(): return lax.psum(kept, axis)]
  transfers between devices with their start and end apart: 5 -> 6, of which waited for: 5 -> 6; matrix products, arithmetic and copies ran while one was open for 4% -> 4% of each run, Pallas kernels for 0% -> 0%
where the time goes in v1:
time: 411 us; the launch traced here: 403 us
  waiting for transfers between devices  253 us (62%)
  local copies, waits for them, and re-layouts  62 us (15%)
  matrix products  54.3 us (13%)
  starting transfers between devices  16 us (4%)
  between operations  14 us (3%)
    psum x1, waiting for transfers between devices, broadcast(): return lax.psum(kept, axis)  121 us
    ppermute x4, waiting for transfers between devices, passed_along(): return lax.ppermute(value, axis, pairs)  111 us
    all_to_all x1, waiting for transfers between devices, on_device(): blocks = lax.all_to_all(blocks, 'col', split_axis=0, concat_axis=0)  21.2 us
    dot_general x2, matrix products, on_device(): jnp.einsum('ijyv,jvw->ijyw', window_cols, right_now, precision=exact_mode)  19.9 us
    dot_general x2, matrix products, on_device(): jnp.einsum('ivw,ijvx->ijwx', left_now, window_rows, precision=exact_mode)  11.5 us
    all_to_all x1, starting transfers between devices, on_device(): blocks = lax.all_to_all(blocks, 'col', split_axis=0, concat_axis=0)  10 us
    unnamed x11, local copies, waits for them, and re-layouts  8.26 us
  transfers between devices with their start and end apart: 6, of which 6 were waited for; matrix products, arithmetic and copies ran while one was open for 4% of the time, Pallas kernels for 0%

profile of v1, /device:TPU:39, one launch (start us, length us, event | category | flops | bytes accessed | tf_op | source)
XLA Modules:
  0.0 403.1 jit_solution(13967096942227960727)
XLA Ops:
  6.5 4.8 %copy.42 = f32[1,1,1,1,1024,1024]{5,4,3,2,1,0:T(8,128)} copy(f32[1,1,1,1,1024,1024]{5,4,3,2,1,0:T(8,128)} %param.21) | data formatting | bytes 8388608
  11.3 1.0 stack.17
  12.3 10.0 %all-to-all-start = ((f32[16,3,1,1,32,128]{5,4,1,3,2,0:T(8,128)}), f32[16,3,1,1,32,128]{5,4,1,3,2,0:T(8,128)S(1)}, u32[]{:S(2)}, u32[]{:S(2)}) async-start(f32[16,3,1,1,32,128]{5,4,1,3,2,0:T(8,128)} %stack.17), calls=%async_computation | async-start | bytes 1572864 | tf_op jit(solution)/shard_map/all_to_all | solution.py:68
  22.4 0.2 fusion.44
  22.7 0.1 fusion.15
  22.8 21.2 %all-to-all-done = f32[16,3,1,1,32,128]{5,4,1,3,2,0:T(8,128)S(1)} async-done(((f32[16,3,1,1,32,128]{5,4,1,3,2,0:T(8,128)}), f32[16,3,1,1,32,128]{5,4,1,3,2,0:T(8,128)S(1)}, u32[]{:S(2)}, u32[]{:S(2)}) %all-to-all-start) | async-done | bytes 786464 | tf_op jit(solution)/shard_map/all_to_all | solution.py:68
  44.1 1.4 fusion.51
  45.5 4.6 %copy.19 = f32[3,128,128]{0,2,1:T(8,128)} copy(f32[3,128,128]{2,1,0:T(8,128)S(1)} %fusion.51) | data formatting | bytes 393216 | tf_op jit(solution)/shard_map/vmap()/dot_general | solution.py:40
  50.1 1.8 gather_fusion
  51.9 0.1 copy.20
  52.0 0.1 select_add_fusion
  52.1 4.6 %copy.21 = f32[3,128,128]{0,2,1:T(8,128)} copy(f32[3,128,128]{2,1,0:T(8,128)S(1)} %select_add_fusion) | data formatting | bytes 393216 | tf_op jit(solution)/shard_map/vmap()/add | solution.py:41
  56.7 1.8 gather_fusion.1
  58.5 0.1 copy.22
  58.6 0.4 fusion.27
  59.0 0.4 fusion.24
  59.4 0.3 fusion.52
  59.7 0.3 fusion.53
  60.1 0.3 fusion.22
  60.4 0.3 fusion.54
  60.7 0.3 fusion.20
  61.1 0.3 fusion.55
  61.4 0.3 fusion.18
  61.7 0.3 convolution_add_fusion
  62.1 0.3 fusion.16
  62.4 0.4 convolution_multiply_fusion
  62.8 0.8 fusion.56
  63.6 5.2 %select_bitcast_fusion = (f32[3,1,512,512]{3,2,0,1:T(8,128)}, f32[3,512,512]{2,1,0:T(8,128)}) fusion(f32[512,512]{1,0:T(8,128)S(1)} %fusion.15, pred[]{:T(512)S(6)} %eq.46, pred[3]{0:T(512)(128)(4,1)S(1)} %get-tuple-element.114, f32[3,128,512]{1,2,0:T(8,128)S(1)} %fusion.56, f32[3,512,128]{2,1,0:T(8,128)S(1)} %bitcast.122), kind=kOutput, calls=%fused_computation.3 | convolution fusion | flops 1210318848 | bytes 8912900 | tf_op jit(solution)/shard_map/vmap()/dot_general | solution.py:44
  68.8 1.8 copy-done
  70.7 5.1 %fusion.3 = f32[512,1024]{1,0:T(8,128)S(1)} fusion(f32[1,1,1024,1024]{3,2,1,0:T(8,128)} %bitcast, f32[3,512,512]{2,1,0:T(8,128)S(1)} %copy-done), kind=kOutput, calls=%fused_computation.12 | convolution fusion | flops 3221225472 | bytes 5242880 | tf_op jit(solution)/shard_map/ivw,ijvx->ijwx/dot_general | solution.py:96
  75.8 1.5 bitcast_dynamic-update-slice_fusion
  77.2 121.3 %all-reduce.2.cloned.1.call-done = f32[3,1,512,512]{3,2,0,1:T(8,128)} async-done(((f32[3,1,512,512]{3,2,0,1:T(8,128)}), f32[3,1,512,512]{3,2,0,1:T(8,128)}) %all-reduce.2.cloned.1.call-update) | async-done | bytes 3145744 | tf_op jit(solution)/shard_map/psum | solution.py:11
  198.5 2.8 select_select_fusion
  201.3 1.6 copy-done.1
  202.9 9.9 %fusion.12 = f32[1,1,1024,512]{2,3,0,1:T(8,128)} fusion(f32[1,1,1024,1024]{3,2,1,0:T(8,128)} %bitcast_dynamic-update-slice_fusion, f32[3,1,512,512]{3,2,0,1:T(8,128)S(1)} %select_select_fusion), kind=kOutput, calls=%fused_computation.24 | convolution fusion | flops 3221225472 | bytes 5242880 | tf_op jit(solution)/shard_map/ijyv,jvw->ijyw/dot_general | solution.py:99
  212.8 2.9 copy.24
  215.7 3.1 constant_dynamic-update-slice_fusion.6
  218.8 1.7 fusion.48
  220.5 0.3 collective-permute-start
  220.7 16.3 %collective-permute-done = f32[1,1,256,1024]{3,2,1,0:T(8,128)S(1)} collective-permute-done((f32[1,1,256,1024]{3,2,1,0:T(8,128)S(1)}, f32[1,1,256,1024]{3,2,1,0:T(8,128)S(1)}, u32[]{:S(2)}, u32[]{:S(2)}) %collective-permute-start) | collective-permute-done | bytes 1048608 | tf_op jit(solution)/shard_map/ppermute | solution.py:17
  237.0 3.5 fusion.11
  240.6 1.5 fusion.50
  242.0 2.5 copy.25
  244.6 2.3 constant_dynamic-update-slice_fusion.5
  246.9 7.2 %collective-permute-done.1 = f32[1,1,256,1024]{2,3,1,0:T(8,128)} collective-permute-done((f32[1,1,256,1024]{2,3,1,0:T(8,128)}, f32[1,1,256,1024]{2,3,1,0:T(8,128)}, u32[]{:S(2)}, u32[]{:S(2)}) %collective-permute-start.1) | collective-permute-done | bytes 1048608 | tf_op jit(solution)/shard_map/ppermute | solution.py:17
  254.1 2.5 copy.26
  256.6 2.3 constant_dynamic-update-slice_fusion.4
  258.9 1.7 fusion.47
  260.6 5.4 %collective-permute-start.2 = (f32[1,1,1024,256]{3,2,1,0:T(8,128)S(1)}, f32[1,1,1024,256]{3,2,1,0:T(8,128)S(1)}, u32[]{:S(2)}, u32[]{:S(2)}) collective-permute-start(f32[1,1,1024,256]{3,2,1,0:T(8,128)S(1)} %get-tuple-element.116), channel_id=1, source_target_pairs={{0,15},{1,0},{2,1},{3,2},{4,3},{5,4},{6,5},{7,6},{8,7},{9,8},{10,9... | collective-permute-start | bytes 3145736 | tf_op jit(solution)/shard_map/ppermute | solution.py:17
  266.0 41.2 %collective-permute-done.2 = f32[1,1,1024,256]{3,2,1,0:T(8,128)S(1)} collective-permute-done((f32[1,1,1024,256]{3,2,1,0:T(8,128)S(1)}, f32[1,1,1024,256]{3,2,1,0:T(8,128)S(1)}, u32[]{:S(2)}, u32[]{:S(2)}) %collective-permute-start.2) | collective-permute-done | bytes 1048608 | tf_op jit(solution)/shard_map/ppermute | solution.py:17
  307.2 8.0 %fusion.10 = f32[1,1,1024,512]{2,3,0,1:T(8,128)S(1)} fusion(f32[1,1,1024,256]{3,2,1,0:T(8,128)S(1)} %collective-permute-done.2, f32[1,1,1024,256]{3,2,1,0:T(8,128)S(1)} %get-tuple-element.115, f32[3,1,512,512]{3,2,0,1:T(8,128)} %copy-done.1), kind=kOutput, calls=%fused_computation.22 | convolution fusion | flops 3221749760 | bytes 5242880 | tf_op jit(solution)/shard_map/ijyv,jvw->ijyw/dot_general | solution.py:118
  315.1 1.5 fusion.49
  316.6 0.2 collective-permute-start.3
  316.8 2.5 copy.27
  319.4 2.3 constant_dynamic-update-slice_fusion.3
  321.7 46.3 %collective-permute-done.3 = f32[1,1,1024,256]{2,3,0,1:T(8,128)} collective-permute-done((f32[1,1,1024,256]{2,3,0,1:T(8,128)}, f32[1,1,1024,256]{2,3,0,1:T(8,128)}, u32[]{:S(2)}, u32[]{:S(2)}) %collective-permute-start.3) | collective-permute-done | bytes 1048608 | tf_op jit(solution)/shard_map/ppermute | solution.py:17
  368.0 2.5 copy.28
  370.5 2.3 constant_dynamic-update-slice_fusion.2
  372.8 6.4 %fusion.13 = f32[1,1,512,1024]{2,3,1,0:T(8,128)} fusion(f32[1,1,1024,1024]{3,2,1,0:T(8,128)} %constant_dynamic-update-slice_fusion.2, f32[3,512,512]{2,1,0:T(8,128)S(1)} %copy-done), kind=kOutput, calls=%fused_computation.25 | convolution fusion | flops 3221225472 | bytes 5242880 | tf_op jit(solution)/shard_map/ivw,ijvx->ijwx/dot_general | solution.py:96
  379.2 1.9 copy.29
  381.1 1.5 constant_dynamic-update-slice_fusion.1
  382.6 10.0 %fusion.14 = f32[1,1,1,1,1024,512]{4,5,3,2,1,0:T(8,128)} fusion(f32[1,1,1024,1024]{3,2,1,0:T(8,128)} %constant_dynamic-update-slice_fusion.1, f32[3,1,512,512]{3,2,0,1:T(8,128)} %copy-done.1), kind=kOutput, calls=%fused_computation.26 | convolution fusion | flops 3221225472 | bytes 5242880 | tf_op jit(solution)/shard_map/ijyv,jvw->ijyw/dot_general | solution.py:99
  392.6 1.9 copy.30
  394.5 1.5 constant_dynamic-update-slice_fusion
  (17 shorter events, 0.2 us)
Async XLA Ops:
  6.5 4.8 %copy-start.3 = (f32[3,1,1,32,128]{4,3,2,1,0:T(8,128)S(1)}, f32[3,1,1,32,128]{4,3,2,1,0:T(8,128)}, u32[]{:S(2)}) copy-start(f32[3,1,1,32,128]{4,3,2,1,0:T(8,128)} %param.22) | copy-start | bytes 147460
  6.5 15.9 %copy-start.4 = (s32[3,16]{1,0:T(4,128)S(1)}, s32[3,16]{1,0:T(4,128)}, u32[]{:S(2)}) copy-start(s32[3,16]{1,0:T(4,128)} %param.23) | copy-start | bytes 580
  12.3 31.7 %all-to-all-start = ((f32[16,3,1,1,32,128]{5,4,1,3,2,0:T(8,128)}), f32[16,3,1,1,32,128]{5,4,1,3,2,0:T(8,128)S(1)}, u32[]{:S(2)}, u32[]{:S(2)}) async-start(f32[16,3,1,1,32,128]{5,4,1,3,2,0:T(8,128)} %stack.17), calls=%async_computation | async-start | bytes 1572864 | tf_op jit(solution)/shard_map/all_to_all | solution.py:68
  22.3 176.1 %all-reduce.2.cloned.1.call-start = ((), (), s32[]{:S(2)}) async-start(), calls=%async_computation.1 | async-start | bytes 6291456 | tf_op jit(solution)/shard_map/psum | solution.py:11
  22.8 40.7 %copy-start.2 = (f32[512,512]{1,0:T(8,128)}, f32[512,512]{1,0:T(8,128)S(1)}, u32[]{:S(2)}) copy-start(f32[512,512]{1,0:T(8,128)S(1)} %fusion.15) | copy-start | bytes 3145732
  68.8 1.9 copy-start
  201.3 1.6 copy-start.1
  220.5 16.6 %collective-permute-start = (f32[1,1,256,1024]{3,2,1,0:T(8,128)S(1)}, f32[1,1,256,1024]{3,2,1,0:T(8,128)S(1)}, u32[]{:S(2)}, u32[]{:S(2)}) collective-permute-start(f32[1,1,256,1024]{3,2,1,0:T(8,128)S(1)} %get-tuple-element.118), channel_id=1, source_target_pairs={{0,240},{16,0},{32,16},{48,32},{64,48},{80,64},{96,80},{112,96},{1... | collective-permute-start | bytes 3145736 | tf_op jit(solution)/shard_map/ppermute | solution.py:17
  242.0 12.1 %collective-permute-start.1 = (f32[1,1,256,1024]{2,3,1,0:T(8,128)}, f32[1,1,256,1024]{2,3,1,0:T(8,128)}, u32[]{:S(2)}, u32[]{:S(2)}) collective-permute-start(f32[1,1,256,1024]{2,3,1,0:T(8,128)} %get-tuple-element.123), channel_id=1, source_target_pairs={{0,16},{16,32},{32,48},{48,64},{64,80},{80,96},{96,112},{112,128},... | collective-permute-start | bytes 3145736 | tf_op jit(solution)/shard_map/ppermute | solution.py:17
  260.6 46.6 %collective-permute-start.2 = (f32[1,1,1024,256]{3,2,1,0:T(8,128)S(1)}, f32[1,1,1024,256]{3,2,1,0:T(8,128)S(1)}, u32[]{:S(2)}, u32[]{:S(2)}) collective-permute-start(f32[1,1,1024,256]{3,2,1,0:T(8,128)S(1)} %get-tuple-element.116), channel_id=1, source_target_pairs={{0,15},{1,0},{2,1},{3,2},{4,3},{5,4},{6,5},{7,6},{8,7},{9,8},{10,9... | collective-permute-start | bytes 3145736 | tf_op jit(solution)/shard_map/ppermute | solution.py:17
  316.6 51.4 %collective-permute-start.3 = (f32[1,1,1024,256]{2,3,0,1:T(8,128)}, f32[1,1,1024,256]{2,3,0,1:T(8,128)}, u32[]{:S(2)}, u32[]{:S(2)}) collective-permute-start(f32[1,1,1024,256]{2,3,0,1:T(8,128)} %get-tuple-element.121), channel_id=1, source_target_pairs={{0,1},{1,2},{2,3},{3,4},{4,5},{5,6},{6,7},{7,8},{8,9},{9,10},{10,1... | collective-permute-start | bytes 3145736 | tf_op jit(solution)/shard_map/ppermute | solution.py:17
Sparse Core Ops, SparseCore 0:
  68.9 129.5 all-reduce.1
